TPU v7x, 32 devices: a whole 2x2x4 slice. The times are simulated.
32 devices in a mesh: mode: 16 (over z, y, x), real: 2 (over core).
Axes of the slice: x: 2, y: 2, z: 4, core: 2. Of those that a mesh axis runs over, the one named last changes fastest.
Arguments:
- input_field: bfloat16 [2, 2, 256, 16384], P(None, 'real', 'mode'), may hold values from -6 to 6
- kerr_coeff: bfloat16 [16, 64, 64], P('mode'), may hold values from -0.375 to 0.375
- block_list: int32 [16, 4], P('mode'), may hold values from 0 to 31
Outputs:
- density: float32 [512, 2, 256, 256], P('mode', None, 'real')
All inputs are finite; a program needn't handle non-finite values.
Results may differ from a plain program's by a relative error of at most 0.0085.
Values may be sent and summed in bfloat16 or wider, within the bound.
A program may use at most 64 MiB of HBM per device.

v0:
```python
import math
import jax
import jax.numpy as jnp
from jax import lax
from jax.sharding import PartitionSpec as P

MB = 8
FT = 128
NT = 16384
FB = 32
kerr_strength = 0.25


def kerr_terms(field_blocks, coeff_group, block_group):
    mode_l = jnp.take(field_blocks, block_group[:, 1], axis=2).astype(jnp.float32)
    mode_m = jnp.take(field_blocks, block_group[:, 2], axis=2).astype(jnp.float32)
    mode_n = jnp.take(field_blocks, block_group[:, 3], axis=2).astype(jnp.float32)
    realiz = field_blocks.shape[1]
    group_size = block_group.shape[0]
    steps_local = field_blocks.shape[4]
    prod_re = (
        mode_m[0][:, :, :, None, :] * mode_n[0][:, :, None, :, :]
        + mode_m[1][:, :, :, None, :] * mode_n[1][:, :, None, :, :]
    )
    prod_im = (
        mode_m[1][:, :, :, None, :] * mode_n[0][:, :, None, :, :]
        - mode_m[0][:, :, :, None, :] * mode_n[1][:, :, None, :, :]
    )
    pairs = (
        jnp.stack([prod_re, prod_im])
        .reshape(2, realiz, group_size, MB * MB, steps_local)
        .astype(jnp.bfloat16)
    )
    weighted = jnp.einsum(
        "kab,crkbt->crkat", coeff_group, pairs, preferred_element_type=jnp.float32
    )
    weighted = weighted.reshape(2, realiz, group_size, MB, MB, steps_local)
    term_re = jnp.sum(
        weighted[0] * mode_l[0][:, :, None] - weighted[1] * mode_l[1][:, :, None], axis=3
    )
    term_im = jnp.sum(
        weighted[0] * mode_l[1][:, :, None] + weighted[1] * mode_l[0][:, :, None], axis=3
    )
    one_hot = (
        block_group[:, 0][:, None] == jnp.arange(field_blocks.shape[2], dtype=jnp.int32)[None, :]
    ).astype(jnp.float32)
    return jnp.einsum(
        "kg,crkpt->crgpt", one_hot, jnp.stack([term_re, term_im]), precision=lax.Precision.HIGHEST
    )


def phase_table(extent, modulus):
    index_a = jnp.arange(extent, dtype=jnp.int32)[:, None]
    index_b = jnp.arange(extent, dtype=jnp.int32)[None, :]
    angle = 2.0 * math.pi / modulus * (index_a * index_b % modulus).astype(jnp.float32)
    return (jnp.cos(angle), -jnp.sin(angle))


def first_pass(table, data):
    table_high = table.astype(jnp.bfloat16)
    table_low = (table - table_high.astype(jnp.float32)).astype(jnp.bfloat16)
    upper = jnp.einsum("kn,rmnj->rmkj", table_high, data, preferred_element_type=jnp.float32)
    return upper + jnp.einsum("kn,rmnj->rmkj", table_low, data, preferred_element_type=jnp.float32)


def second_pass(table, data):
    return jnp.einsum("jn,rmkn->rmjk", table, data, precision=lax.Precision.HIGH)


def transform(by_mode):
    realiz = by_mode.shape[1]
    local_modes = by_mode.shape[2]
    signal = by_mode.reshape(2, realiz, local_modes, FT, FT)
    four_re, four_im = phase_table(FT, FT)
    twist_re, twist_im = phase_table(FT, NT)
    half_re = first_pass(four_re, signal[0]) - first_pass(four_im, signal[1])
    half_im = first_pass(four_re, signal[1]) + first_pass(four_im, signal[0])
    turned_re = half_re * twist_re - half_im * twist_im
    turned_im = half_re * twist_im + half_im * twist_re
    out_re = (second_pass(four_re, turned_re) - second_pass(four_im, turned_im)) / FT
    out_im = (second_pass(four_re, turned_im) + second_pass(four_im, turned_re)) / FT
    return jnp.stack([out_re, out_im]).astype(jnp.bfloat16)


def gram_parts(rows_part, cols_part):
    quarters = jnp.einsum(
        "crpbf,drqbf->bcdpq", rows_part, cols_part, preferred_element_type=jnp.float32
    )
    return jnp.stack(
        [quarters[:, 0, 0] + quarters[:, 1, 1], quarters[:, 1, 0] - quarters[:, 0, 1]], axis=1
    )


def shards(input_field, kerr_coeff, block_list):
    timed = lax.all_to_all(input_field, "mode", split_axis=3, concat_axis=2, tiled=True)
    realiz = timed.shape[1]
    width = timed.shape[2]
    steps_local = timed.shape[3]
    field_blocks = timed.reshape(2, realiz, width // MB, MB, steps_local)
    initial = jnp.zeros(field_blocks.shape, jnp.float32)
    running = initial
    coeff_piece = lax.all_gather(kerr_coeff, "mode", axis=0, tiled=True)
    block_piece = lax.all_gather(block_list, "mode", axis=0, tiled=True)
    block_count = block_piece.shape[0]
    coeff_groups = coeff_piece.reshape(
        block_count // 8, 8, coeff_piece.shape[1], coeff_piece.shape[2]
    )
    block_groups = block_piece.reshape(block_count // 8, 8, 4)

    def one_group(carried, groups):
        return (carried + kerr_terms(field_blocks, groups[0], groups[1]), None)

    running, unused = lax.scan(one_group, running, (coeff_groups, block_groups))
    kerr_sum = running
    kerr_sum = kerr_sum.reshape(2, realiz, width, steps_local)
    base = timed.astype(jnp.float32)
    stepped = jnp.stack(
        [base[0] - kerr_strength * kerr_sum[1], base[1] + kerr_strength * kerr_sum[0]]
    ).astype(jnp.bfloat16)
    by_mode = lax.all_to_all(stepped, "mode", split_axis=2, concat_axis=3, tiled=True)
    spectrum = transform(by_mode)
    banded = lax.all_to_all(spectrum, "mode", split_axis=3, concat_axis=2, tiled=True)
    bands_dev = banded.shape[3] * FT // FB
    spec_bands = banded.reshape(2, realiz, width, bands_dev, FB)
    scale = 1.0 / (FB * realiz * lax.axis_size("real"))
    row_count = width // lax.axis_size("real")
    row_first = lax.axis_index("real") * row_count
    shard_piece = lax.all_gather(spec_bands, "real", axis=1, tiled=True)
    own_part = lax.dynamic_slice_in_dim(shard_piece, row_first, row_count, 2)
    return gram_parts(own_part, shard_piece) * scale


def solution(mesh):
    return jax.shard_map(
        shards,
        mesh=mesh,
        in_specs=(P(None, "real", "mode", None), P("mode", None, None), P("mode", None)),
        out_specs=P("mode", None, "real", None),
        check_vma=False,
    )
```

profile of v0, /device:TPU:0, one launch (start us, length us, event | category | flops | bytes accessed | tf_op | source)
XLA Modules:
  0.0 297.2 jit_solution(920240638021889750)
XLA Ops:
  6.5 15.9 %copy.145 = bf16[2,1,16,16384]{2,0,1,3:T(2,128)(2,1)} copy(bf16[2,1,16,16384]{3,2,1,0:T(8,128)(2,1)} %param.7) | data formatting | bytes 2097152 | tf_op args[0]
  22.5 11.2 %reshape.574 = bf16[16,2,16384]{2,1,0:T(2,128)(2,1)} reshape(bf16[16384,1,2,16]{3,2,1,0:T(2,128)(2,1)} %bitcast.267) | data formatting | bytes 2097152
  33.7 8.5 %all-to-all-start = ((bf16[16,2,16384]{2,1,0:T(2,128)(2,1)}), bf16[16,2,16384]{2,1,0:T(2,128)(2,1)S(1)}, u32[]{:S(2)}, u32[]{:S(2)}) async-start(bf16[16,2,16384]{2,1,0:T(2,128)(2,1)} %reshape.574), calls=%async_computation | async-start | bytes 2097152 | tf_op jit(solution)/shard_map/all_to_all | solution.py:95
  42.2 50.9 %all-gather = s32[16,1,4]{2,1,0:T(1,128)S(1)} all-gather(s32[1,1,4]{2,1,0:T(1,128)S(1)} %bitcast.278), channel_id=1, replica_groups=mesh['mode'=16,'real'=2] {'mode'}, dimensions={0}, use_global_device_ids=true | all-gather | bytes 272 | tf_op jit(solution)/shard_map/all_gather | solution.py:103
  93.2 38.7 %all_gather.10 = bf16[16,64,64]{2,1,0:T(8,128)(2,1)S(1)} all-gather(bf16[1,64,64]{2,1,0:T(8,128)(2,1)S(1)} %copy-done.4), channel_id=1, replica_groups=mesh['mode'=16,'real'=2] {'mode'}, dimensions={0}, use_global_device_ids=true | all-gather | bytes 139264 | tf_op jit(solution)/shard_map/all_gather | solution.py:102
  131.8 7.4 %reshape.575 = bf16[16384,1,2,16]{3,2,1,0:T(2,128)(2,1)} reshape(bf16[16,2,16384]{2,1,0:T(2,128)(2,1)S(1)} %all-to-all-done) | data formatting | bytes 2097152
  139.2 17.7 %copy.200 = bf16[2,1,16,16,1024]{4,2,3,0,1:T(8,128)(2,1)S(1)} copy(bf16[2,1,16,16,1024]{2,0,4,3,1:T(2,128)(2,1)} %bitcast.265) | data formatting | bytes 2097152 | tf_op jit(solution)/shard_map/all_to_all | solution.py:95
  156.9 12.7 %copy.197 = bf16[2,1,16,16,1024]{4,3,2,0,1:T(8,128)(2,1)} copy(bf16[2,1,16,16,1024]{2,0,4,3,1:T(2,128)(2,1)} %bitcast.266) | data formatting | bytes 2097152 | tf_op jit(solution)/shard_map/all_to_all | solution.py:95
  169.6 23.4 %while.11 = (s32[]{:T(128)}, f32[2,1,32,8,1024]{4,2,3,0,1:T(8,128)S(1)}, s32[2,8,4]{1,2,0:T(4,128)S(1)}, bf16[2,1,32,8,1024]{4,3,2,1,0:T(8,128)(2,1)S(1)}, bf16[...) while((s32[]{:T(128)}, f32[2,1,32,8,1024]{4,2,3,0,1:T(8,128)S(1)}, ...), condition=%wide.region_3.5_spmd.clone, body=%wide.region_0.4_spmd.clone.sunk | while | flops 198970768 | bytes 36058028 | solution.py:113
  169.7 0.9 copy-done
  170.6 1.8 gather_fusion.2
  172.4 1.8 gather_fusion.1
  174.2 1.8 gather_fusion
  176.4 0.6 fusion.157
  177.0 0.7 convolution_bitcast_fusion.3
  177.7 1.5 subtract_reduce_fusion.2
  179.6 1.7 bitcast_add_fusion.2
  181.4 0.9 copy-done
  182.3 1.8 gather_fusion.2
  184.1 1.8 gather_fusion.1
  185.9 1.8 gather_fusion
  188.1 0.6 fusion.157
  188.8 0.7 convolution_bitcast_fusion.3
  189.5 1.5 subtract_reduce_fusion.2
  191.4 1.7 bitcast_add_fusion.2
  193.1 1.2 copy.152
  194.3 0.2 bitcast_convert_fusion
  194.8 0.6 copy.147
  195.4 0.6 copy.153
  196.1 0.5 fusion.37
  196.7 2.0 copy.155
  198.7 3.7 %all-to-all-start.1 = ((bf16[2,1,256,1024]{3,0,1,2:T(2,128)(2,1)}), bf16[2,1,256,1024]{3,0,1,2:T(2,128)(2,1)S(1)}, u32[]{:S(2)}, u32[]{:S(2)}) async-start(bf16[2,1,256,1024]{3,0,1,2:T(2,128)(2,1)} %copy.155), calls=%async_computation.1 | async-start | bytes 2097152 | tf_op jit(solution)/shard_map/all_to_all | solution.py:120
  202.6 0.3 fusion.78
  203.0 0.3 sine_negate_fusion
  203.3 14.6 %all-to-all-done.1 = bf16[2,1,256,1024]{3,0,1,2:T(2,128)(2,1)S(1)} async-done(((bf16[2,1,256,1024]{3,0,1,2:T(2,128)(2,1)}), bf16[2,1,256,1024]{3,0,1,2:T(2,128)(2,1)S(1)}, u32[]{:S(2)}, u32[]{:S(2)}) %all-to-all-start.1) | async-done | bytes 1048608 | tf_op jit(solution)/shard_map/all_to_all | solution.py:120
  217.9 0.3 copy.156
  218.2 0.9 fusion.137
  219.1 0.3 copy.160
  219.6 0.5 fusion.65
  220.2 0.5 fusion.85
  220.7 1.1 copy.157
  221.8 1.3 reshape.509
  223.1 0.5 fusion.83
  223.6 0.5 fusion.67
  224.2 0.5 convolution_add_fusion.2
  224.7 0.5 convolution_add_fusion.4
  225.3 0.5 fusion.25
  225.8 0.5 fusion.27
  226.4 1.2 fusion.39
  227.6 1.2 fusion.43
  228.8 1.2 fusion.30
  229.9 1.2 fusion.31
  231.2 1.0 copy.173
  232.2 21.6 %all_to_all.45 = bf16[2,1,16,128,128]{4,2,1,0,3:T(8,128)(2,1)S(1)} all-to-all(bf16[2,1,16,128,128]{4,2,1,0,3:T(8,128)(2,1)S(1)} %copy.173), channel_id=1, replica_groups=mesh['mode'=16,'real'=2] {'mode'}, dimensions={3} | all-to-all | bytes 2097152 | tf_op jit(solution)/shard_map/all_to_all | solution.py:122
  253.8 0.4 copy.208
  254.2 0.3 copy.175
  254.5 3.2 %reshape.513 = bf16[2,1,256,32,32]{4,3,2,0,1:T(8,128)(2,1)} reshape(bf16[2,1,16,16,8,128]{5,4,3,2,0,1:T(8,128)(2,1)S(1)} %copy.175) | data formatting | bytes 2097152 | tf_op jit(solution)/shard_map/reshape | solution.py:124
  257.7 5.2 %copy.176 = bf16[2,1,256,32,32]{2,4,1,0,3:T(8,128)(2,1)} copy(bf16[2,1,256,32,32]{4,3,2,0,1:T(8,128)(2,1)} %reshape.513) | data formatting | bytes 2097152 | tf_op jit(solution)/shard_map/reshape | solution.py:124
  263.0 9.0 %all-gather.3.cloned.1.call-done = bf16[2,2,256,32,32]{2,4,1,0,3:T(8,128)(2,1)} async-done(((bf16[2,1,256,32,32]{2,4,1,0,3:T(8,128)(2,1)}), bf16[2,2,256,32,32]{2,4,1,0,3:T(8,128)(2,1)}) %all-gather.3.cloned.1.call-update) | async-done | bytes 2097168 | tf_op jit(solution)/shard_map/all_gather | solution.py:128
  272.0 4.2 %convolution_bitcast_fusion.1 = f32[32,2,2,128,256]{3,4,1,2,0:T(8,128)S(1)} fusion(bf16[2,2,256,32,32]{2,4,1,0,3:T(8,128)(2,1)} %all-gather.3.cloned.1.call-done, s32[]{:T(128)S(6)} %select_n.66), kind=kOutput, calls=%fused_computation.52 | convolution fusion | flops 536870912 | bytes 19922948 | tf_op jit(solution)/shard_map/crpbf,drqbf->bcdpq/dot_general | solution.py:86
  276.2 0.6 fusion.18
  276.9 0.6 fusion.20
  277.5 3.9 %maximum_multiply_fusion = f32[32,2,128,256]{2,3,0,1:T(8,128)} fusion(f32[32,1,128,256]{2,3,0,1:T(8,128)S(1)} %fusion.18, f32[32,1,128,256]{2,3,0,1:T(8,128)S(1)} %fusion.20), kind=kLoop, calls=%fused_computation.53 | loop fusion | flops 4194304 | bytes 16777216 | tf_op jit(solution)/shard_map/mul | solution.py:130
  281.4 8.9 %copy.179 = f32[32,2,128,256]{3,2,1,0:T(8,128)} copy(f32[32,2,128,256]{2,3,0,1:T(8,128)} %maximum_multiply_fusion) | data formatting | bytes 16777216 | tf_op jit(solution)/shard_map/mul | solution.py:130
  (51 shorter events, 2.6 us)
Async XLA Ops:
  33.7 8.5 %copy-start.5 = (s32[1,4]{1,0:T(1,128)S(1)}, s32[1,4]{1,0:T(1,128)}, u32[]{:S(2)}) copy-start(s32[1,4]{1,0:T(1,128)} %param.9) | copy-start | bytes 52
  33.7 59.5 %copy-start.4 = (bf16[1,64,64]{2,1,0:T(8,128)(2,1)S(1)}, bf16[1,64,64]{2,1,0:T(8,128)(2,1)}, u32[]{:S(2)}) copy-start(bf16[1,64,64]{2,1,0:T(8,128)(2,1)} %param.8) | copy-start | bytes 24580
  33.7 98.1 %all-to-all-start = ((bf16[16,2,16384]{2,1,0:T(2,128)(2,1)}), bf16[16,2,16384]{2,1,0:T(2,128)(2,1)S(1)}, u32[]{:S(2)}, u32[]{:S(2)}) async-start(bf16[16,2,16384]{2,1,0:T(2,128)(2,1)} %reshape.574), calls=%async_computation | async-start | bytes 2097152 | tf_op jit(solution)/shard_map/all_to_all | solution.py:95
  169.6 1.0 copy-start
  179.6 1.7 copy-start.1
  181.4 1.0 copy-start
  191.3 1.7 copy-start.1
  193.1 1.2 copy-start.2
  198.7 19.2 %all-to-all-start.1 = ((bf16[2,1,256,1024]{3,0,1,2:T(2,128)(2,1)}), bf16[2,1,256,1024]{3,0,1,2:T(2,128)(2,1)S(1)}, u32[]{:S(2)}, u32[]{:S(2)}) async-start(bf16[2,1,256,1024]{3,0,1,2:T(2,128)(2,1)} %copy.155), calls=%async_computation.1 | async-start | bytes 2097152 | tf_op jit(solution)/shard_map/all_to_all | solution.py:120
  202.4 69.6 %all-gather.3.cloned.1.call-start = ((), (), s32[]{:S(2)}) async-start(), calls=%async_computation.3 | async-start | bytes 3145728 | tf_op jit(solution)/shard_map/all_gather | solution.py:128
  219.6 1.1 copy-start.3
Sparse Core Ops, SparseCore 0:
  263.1 8.8 all-gather.2
where the time goes:
time: 300 us; the launch traced here: 297 us
  blocking collectives  111 us (37%)
  local copies, waits for them, and re-layouts  106 us (35%)
  waiting for transfers between devices  23.6 us (8%)
  matrix products  18.1 us (6%)
  between operations  13.7 us (5%)
  starting transfers between devices  12.3 us (4%)
  other arithmetic  11.5 us (4%)
    all_gather x1, blocking collectives, shards(): block_piece = lax.all_gather(block_list, 'mode', axis=0, tiled=True)  50.9 us
    all_gather x1, blocking collectives, shards(): coeff_piece = lax.all_gather(kerr_coeff, 'mode', axis=0, tiled=True)  38.7 us
    unnamed x12, local copies, waits for them, and re-layouts  34.7 us
    all_to_all x2, local copies, waits for them, and re-layouts, shards(): lax.all_to_all(input_field, 'mode', split_axis=3, concat_axis=2, tiled=True)  30.4 us
    all_to_all x1, blocking collectives, shards(): lax.all_to_all(spectrum, 'mode', split_axis=3, concat_axis=2, tiled=True)  21.6 us
    all_to_all x1, waiting for transfers between devices, shards(): lax.all_to_all(stepped, 'mode', split_axis=2, concat_axis=3, tiled=True)  14.6 us
    all_gather x1, waiting for transfers between devices, shards(): shard_piece = lax.all_gather(spec_bands, 'real', axis=1, tiled=True)  9 us
    mul x1, local copies, waits for them, and re-layouts, shards(): return gram_parts(own_part, shard_piece) * scale  8.94 us
  transfers between devices with their start and end apart: 3, of which 2 were waited for; matrix products, arithmetic and copies ran while one was open for 0% of the time, Pallas kernels for 0%

commit v1 on v0

--- a/solution.py
+++ b/solution.py
@@ -99,7 +99,35 @@
     field_blocks = timed.reshape(2, realiz, width // MB, MB, steps_local)
     initial = jnp.zeros(field_blocks.shape, jnp.float32)
     running = initial
-    coeff_piece = lax.all_gather(kerr_coeff, "mode", axis=0, tiled=True)
+
+    def load_local_data_all(local_array):
+        all_values, frame_out, vec_out = (
+            lax.axis_size("mode"),
+            lax.axis_index("mode"),
+            local_array.shape[0],
+        )
+        trail = [q * all_values if jj == 0 else q for jj, q in enumerate(local_array.shape)]
+        piece_now = lax.dynamic_update_slice_in_dim(
+            jnp.zeros(trail, local_array.dtype), local_array, frame_out * vec_out, axis=0
+        )
+        passed = row_out = local_array
+        for i0 in range(1, all_values // 2 + 1):
+            passed = lax.ppermute(
+                passed, "mode", [(jj, (jj + 1) % all_values) for jj in range(all_values)]
+            )
+            piece_now = lax.dynamic_update_slice_in_dim(
+                piece_now, passed, (frame_out - i0) % all_values * vec_out, axis=0
+            )
+            if 2 * i0 < all_values:
+                row_out = lax.ppermute(
+                    row_out, "mode", [(jj, (jj - 1) % all_values) for jj in range(all_values)]
+                )
+                piece_now = lax.dynamic_update_slice_in_dim(
+                    piece_now, row_out, (frame_out + i0) % all_values * vec_out, axis=0
+                )
+        return piece_now
+
+    coeff_piece = load_local_data_all(kerr_coeff)
     block_piece = lax.all_gather(block_list, "mode", axis=0, tiled=True)
     block_count = block_piece.shape[0]
     coeff_groups = coeff_piece.reshape(

time: 300 us -> 315 us (1.050)
  blocking collectives: 111 us -> 67.1 us
  starting transfers between devices: 12.3 us -> 48.9 us
  waiting for transfers between devices: 23.6 us -> 45.6 us
    all_gather x1 -> x0, blocking collectives: 38.7 us -> none  [shards(): coeff_piece = lax.all_gather(kerr_coeff, 'mode', axis=0, tiled=True)]
    ppermute x0 -> x15, starting transfers between devices: none -> 36.5 us  [the longest x7 36.2 us: load_local_data_all(): lax.ppermute(row_out, 'mode', [(jj, (jj - 1) % all_values) for jj in rang...]
    ppermute x0 -> x15, waiting for transfers between devices: none -> 22 us  [the longest x8 14.6 us: load_local_data_all(): lax.ppermute(passed, 'mode', [(jj, (jj + 1) % all_values) for jj in range...]
    all_gather x1, blocking collectives: 50.9 us -> 45.5 us  [shards(): block_piece = lax.all_gather(block_list, 'mode', axis=0, tiled=True)]
  transfers between devices with their start and end apart: 3 -> 18, of which waited for: 2 -> 9; matrix products, arithmetic and copies ran while one was open for 0% -> 0% of each run, Pallas kernels for 0% -> 0%
where the time goes in v1:
time: 315 us; the launch traced here: 312 us
  local copies, waits for them, and re-layouts  107 us (34%)
  blocking collectives  67.1 us (21%)
  starting transfers between devices  48.9 us (16%)
  waiting for transfers between devices  45.6 us (14%)
  matrix products  18.1 us (6%)
  between operations  13.9 us (4%)
  other arithmetic  11.6 us (4%)
    all_gather x1, blocking collectives, shards(): block_piece = lax.all_gather(block_list, 'mode', axis=0, tiled=True)  45.5 us
    ppermute x7, starting transfers between devices, load_local_data_all(): lax.ppermute(row_out, 'mode', [(jj, (jj - 1) % all_values) for jj in rang...  36.2 us
    unnamed x12, local copies, waits for them, and re-layouts  34.7 us
    all_to_all x2, local copies, waits for them, and re-layouts, shards(): lax.all_to_all(input_field, 'mode', split_axis=3, concat_axis=2, tiled=True)  30.4 us
    all_to_all x1, blocking collectives, shards(): lax.all_to_all(spectrum, 'mode', split_axis=3, concat_axis=2, tiled=True)  21.6 us
    ppermute x8, waiting for transfers between devices, load_local_data_all(): lax.ppermute(passed, 'mode', [(jj, (jj + 1) % all_values) for jj in range...  14.6 us
    all_to_all x1, waiting for transfers between devices, shards(): lax.all_to_all(stepped, 'mode', split_axis=2, concat_axis=3, tiled=True)  14.6 us
    all_gather x1, waiting for transfers between devices, shards(): shard_piece = lax.all_gather(spec_bands, 'real', axis=1, tiled=True)  9 us
  transfers between devices with their start and end apart: 18, of which 9 were waited for; matrix products, arithmetic and copies ran while one was open for 0% of the time, Pallas kernels for 0%

profile of v1, /device:TPU:0, one launch (start us, length us, event | category | flops | bytes accessed | tf_op | source)
XLA Modules:
  0.0 312.1 jit_solution(2706726568243350774)
XLA Ops:
  6.5 15.9 %copy.145 = bf16[2,1,16,16384]{2,0,1,3:T(2,128)(2,1)} copy(bf16[2,1,16,16384]{3,2,1,0:T(8,128)(2,1)} %param.7) | data formatting | bytes 2097152 | tf_op args[0]
  22.5 11.2 %reshape.574 = bf16[16,2,16384]{2,1,0:T(2,128)(2,1)} reshape(bf16[16384,1,2,16]{3,2,1,0:T(2,128)(2,1)} %bitcast.267) | data formatting | bytes 2097152
  33.7 8.5 %all-to-all-start = ((bf16[16,2,16384]{2,1,0:T(2,128)(2,1)}), bf16[16,2,16384]{2,1,0:T(2,128)(2,1)S(1)}, u32[]{:S(2)}, u32[]{:S(2)}) async-start(bf16[16,2,16384]{2,1,0:T(2,128)(2,1)} %reshape.574), calls=%async_computation | async-start | bytes 2097152 | tf_op jit(solution)/shard_map/all_to_all | solution.py:95
  42.2 5.6 %collective-permute-start.1 = (bf16[1,64,64]{2,1,0:T(8,128)(2,1)S(1)}, bf16[1,64,64]{2,1,0:T(8,128)(2,1)S(1)}, u32[]{:S(2)}, u32[]{:S(2)}) collective-permute-start(bf16[1,64,64]{2,1,0:T(8,128)(2,1)S(1)} %copy-done.4), channel_id=1, source_target_pairs={{0,30},{2,0},{4,2},{6,4},{8,6},{10,8},{12,10},{14,12},{16,14},{18,... | collective-permute-start | bytes 24584 | tf_op jit(solution)/shard_map/ppermute | solution.py:122
  48.0 45.5 %all-gather = s32[16,1,4]{2,1,0:T(1,128)S(1)} all-gather(s32[1,1,4]{2,1,0:T(1,128)S(1)} %bitcast.278), channel_id=1, replica_groups=mesh['mode'=16,'real'=2] {'mode'}, dimensions={0}, use_global_device_ids=true | all-gather | bytes 272 | tf_op jit(solution)/shard_map/all_gather | solution.py:131
  93.6 1.7 collective-permute-start.3
  95.7 1.7 collective-permute-done.3
  97.4 5.3 %collective-permute-start.5 = (bf16[1,64,64]{2,1,0:T(8,128)(2,1)S(1)}, bf16[1,64,64]{2,1,0:T(8,128)(2,1)S(1)}, u32[]{:S(2)}, u32[]{:S(2)}) collective-permute-start(bf16[1,64,64]{2,1,0:T(8,128)(2,1)S(1)} %collective-permute-done.3), channel_id=1, source_target_pairs={{0,30},{2,0},{4,2},{6,4},{8,6},{10,8},{12,10},{14,12},{16,14},{18,... | collective-permute-start | bytes 24584 | tf_op jit(solution)/shard_map/ppermute | solution.py:122
  102.7 1.4 collective-permute-done.5
  104.1 5.9 %collective-permute-start.7 = (bf16[1,64,64]{2,1,0:T(8,128)(2,1)S(1)}, bf16[1,64,64]{2,1,0:T(8,128)(2,1)S(1)}, u32[]{:S(2)}, u32[]{:S(2)}) collective-permute-start(bf16[1,64,64]{2,1,0:T(8,128)(2,1)S(1)} %collective-permute-done.5), channel_id=1, source_target_pairs={{0,30},{2,0},{4,2},{6,4},{8,6},{10,8},{12,10},{14,12},{16,14},{18,... | collective-permute-start | bytes 24584 | tf_op jit(solution)/shard_map/ppermute | solution.py:122
  110.1 1.4 collective-permute-done.7
  111.5 5.9 %collective-permute-start.9 = (bf16[1,64,64]{2,1,0:T(8,128)(2,1)S(1)}, bf16[1,64,64]{2,1,0:T(8,128)(2,1)S(1)}, u32[]{:S(2)}, u32[]{:S(2)}) collective-permute-start(bf16[1,64,64]{2,1,0:T(8,128)(2,1)S(1)} %collective-permute-done.7), channel_id=1, source_target_pairs={{0,30},{2,0},{4,2},{6,4},{8,6},{10,8},{12,10},{14,12},{16,14},{18,... | collective-permute-start | bytes 24584 | tf_op jit(solution)/shard_map/ppermute | solution.py:122
  117.4 1.4 collective-permute-done.9
  118.8 5.9 %collective-permute-start.11 = (bf16[1,64,64]{2,1,0:T(8,128)(2,1)S(1)}, bf16[1,64,64]{2,1,0:T(8,128)(2,1)S(1)}, u32[]{:S(2)}, u32[]{:S(2)}) collective-permute-start(bf16[1,64,64]{2,1,0:T(8,128)(2,1)S(1)} %collective-permute-done.9), channel_id=1, source_target_pairs={{0,30},{2,0},{4,2},{6,4},{8,6},{10,8},{12,10},{14,12},{16,14},{18,... | collective-permute-start | bytes 24584 | tf_op jit(solution)/shard_map/ppermute | solution.py:122
  124.7 1.4 collective-permute-done.11
  126.1 5.9 %collective-permute-start.13 = (bf16[1,64,64]{2,1,0:T(8,128)(2,1)S(1)}, bf16[1,64,64]{2,1,0:T(8,128)(2,1)S(1)}, u32[]{:S(2)}, u32[]{:S(2)}) collective-permute-start(bf16[1,64,64]{2,1,0:T(8,128)(2,1)S(1)} %collective-permute-done.11), channel_id=1, source_target_pairs={{0,30},{2,0},{4,2},{6,4},{8,6},{10,8},{12,10},{14,12},{16,14},{18,... | collective-permute-start | bytes 24584 | tf_op jit(solution)/shard_map/ppermute | solution.py:122
  132.1 7.3 %collective-permute-done.12 = bf16[1,64,64]{2,1,0:T(8,128)(2,1)S(1)} collective-permute-done((bf16[1,64,64]{2,1,0:T(8,128)(2,1)S(1)}, bf16[1,64,64]{2,1,0:T(8,128)(2,1)S(1)}, u32[]{:S(2)}, u32[]{:S(2)}) %collective-permute-start.12) | collective-permute-done | bytes 8224 | tf_op jit(solution)/shard_map/ppermute | solution.py:115
  139.4 7.3 %collective-permute-done.14 = bf16[1,64,64]{2,1,0:T(8,128)(2,1)S(1)} collective-permute-done((bf16[1,64,64]{2,1,0:T(8,128)(2,1)S(1)}, bf16[1,64,64]{2,1,0:T(8,128)(2,1)S(1)}, u32[]{:S(2)}, u32[]{:S(2)}) %collective-permute-start.14) | collective-permute-done | bytes 8224 | tf_op jit(solution)/shard_map/ppermute | solution.py:115
  146.7 7.4 %reshape.575 = bf16[16384,1,2,16]{3,2,1,0:T(2,128)(2,1)} reshape(bf16[16,2,16384]{2,1,0:T(2,128)(2,1)S(1)} %all-to-all-done) | data formatting | bytes 2097152
  154.1 17.7 %copy.200 = bf16[2,1,16,16,1024]{4,2,3,0,1:T(8,128)(2,1)S(1)} copy(bf16[2,1,16,16,1024]{2,0,4,3,1:T(2,128)(2,1)} %bitcast.265) | data formatting | bytes 2097152 | tf_op jit(solution)/shard_map/all_to_all | solution.py:95
  171.8 12.7 %copy.197 = bf16[2,1,16,16,1024]{4,3,2,0,1:T(8,128)(2,1)} copy(bf16[2,1,16,16,1024]{2,0,4,3,1:T(2,128)(2,1)} %bitcast.266) | data formatting | bytes 2097152 | tf_op jit(solution)/shard_map/all_to_all | solution.py:95
  184.5 23.4 %while.11 = (s32[]{:T(128)}, f32[2,1,32,8,1024]{4,2,3,0,1:T(8,128)S(1)}, s32[2,8,4]{1,2,0:T(4,128)S(1)}, bf16[2,1,32,8,1024]{4,3,2,1,0:T(8,128)(2,1)S(1)}, bf16[...) while((s32[]{:T(128)}, f32[2,1,32,8,1024]{4,2,3,0,1:T(8,128)S(1)}, ...), condition=%wide.region_3.5_spmd.clone, body=%wide.region_0.4_spmd.clone.sunk | while | flops 198970768 | bytes 36058028 | solution.py:141
  184.5 0.9 copy-done
  185.5 1.8 gather_fusion.2
  187.2 1.8 gather_fusion.1
  189.0 1.8 gather_fusion
  191.2 0.6 fusion.157
  191.9 0.7 convolution_bitcast_fusion.3
  192.6 1.5 subtract_reduce_fusion.2
  194.5 1.7 bitcast_add_fusion.2
  196.3 0.9 copy-done
  197.2 1.8 gather_fusion.2
  199.0 1.8 gather_fusion.1
  200.8 1.8 gather_fusion
  203.0 0.6 fusion.157
  203.6 0.7 convolution_bitcast_fusion.3
  204.3 1.5 subtract_reduce_fusion.2
  206.2 1.7 bitcast_add_fusion.2
  207.9 1.2 copy.152
  209.7 0.6 copy.147
  210.3 0.6 copy.153
  211.5 2.0 copy.155
  213.6 3.7 %all-to-all-start.1 = ((bf16[2,1,256,1024]{3,0,1,2:T(2,128)(2,1)}), bf16[2,1,256,1024]{3,0,1,2:T(2,128)(2,1)S(1)}, u32[]{:S(2)}, u32[]{:S(2)}) async-start(bf16[2,1,256,1024]{3,0,1,2:T(2,128)(2,1)} %copy.155), calls=%async_computation.1 | async-start | bytes 2097152 | tf_op jit(solution)/shard_map/all_to_all | solution.py:148
  218.2 14.6 %all-to-all-done.1 = bf16[2,1,256,1024]{3,0,1,2:T(2,128)(2,1)S(1)} async-done(((bf16[2,1,256,1024]{3,0,1,2:T(2,128)(2,1)}), bf16[2,1,256,1024]{3,0,1,2:T(2,128)(2,1)S(1)}, u32[]{:S(2)}, u32[]{:S(2)}) %all-to-all-start.1) | async-done | bytes 1048608 | tf_op jit(solution)/shard_map/all_to_all | solution.py:148
  233.1 0.9 fusion.137
  235.6 1.1 copy.157
  236.7 1.3 reshape.509
  237.9 0.5 fusion.83
  240.1 0.5 fusion.25
  240.7 0.5 fusion.27
  241.2 1.2 fusion.39
  242.4 1.2 fusion.43
  243.6 1.2 fusion.30
  244.8 1.2 fusion.31
  246.1 1.0 copy.173
  247.1 21.6 %all_to_all.45 = bf16[2,1,16,128,128]{4,2,1,0,3:T(8,128)(2,1)S(1)} all-to-all(bf16[2,1,16,128,128]{4,2,1,0,3:T(8,128)(2,1)S(1)} %copy.173), channel_id=1, replica_groups=mesh['mode'=16,'real'=2] {'mode'}, dimensions={3} | all-to-all | bytes 2097152 | tf_op jit(solution)/shard_map/all_to_all | solution.py:150
  269.3 3.2 %reshape.513 = bf16[2,1,256,32,32]{4,3,2,0,1:T(8,128)(2,1)} reshape(bf16[2,1,16,16,8,128]{5,4,3,2,0,1:T(8,128)(2,1)S(1)} %copy.175) | data formatting | bytes 2097152 | tf_op jit(solution)/shard_map/reshape | solution.py:152
  272.5 5.2 %copy.176 = bf16[2,1,256,32,32]{2,4,1,0,3:T(8,128)(2,1)} copy(bf16[2,1,256,32,32]{4,3,2,0,1:T(8,128)(2,1)} %reshape.513) | data formatting | bytes 2097152 | tf_op jit(solution)/shard_map/reshape | solution.py:152
  277.8 9.0 %all-gather.3.cloned.1.call-done = bf16[2,2,256,32,32]{2,4,1,0,3:T(8,128)(2,1)} async-done(((bf16[2,1,256,32,32]{2,4,1,0,3:T(8,128)(2,1)}), bf16[2,2,256,32,32]{2,4,1,0,3:T(8,128)(2,1)}) %all-gather.3.cloned.1.call-update) | async-done | bytes 2097168 | tf_op jit(solution)/shard_map/all_gather | solution.py:156
  286.8 4.2 %convolution_bitcast_fusion.1 = f32[32,2,2,128,256]{3,4,1,2,0:T(8,128)S(1)} fusion(bf16[2,2,256,32,32]{2,4,1,0,3:T(8,128)(2,1)} %all-gather.3.cloned.1.call-done, s32[]{:T(128)S(6)} %select_n.207), kind=kOutput, calls=%fused_computation.52 | convolution fusion | flops 536870912 | bytes 19922948 | tf_op jit(solution)/shard_map/crpbf,drqbf->bcdpq/dot_general | solution.py:86
  291.1 0.6 fusion.18
  291.7 0.6 fusion.20
  292.4 3.9 %maximum_multiply_fusion = f32[32,2,128,256]{2,3,0,1:T(8,128)} fusion(f32[32,1,128,256]{2,3,0,1:T(8,128)S(1)} %fusion.18, f32[32,1,128,256]{2,3,0,1:T(8,128)S(1)} %fusion.20), kind=kLoop, calls=%fused_computation.53 | loop fusion | flops 4194304 | bytes 16777216 | tf_op jit(solution)/shard_map/mul | solution.py:158
  296.3 8.9 %copy.179 = f32[32,2,128,256]{3,2,1,0:T(8,128)} copy(f32[32,2,128,256]{2,3,0,1:T(8,128)} %maximum_multiply_fusion) | data formatting | bytes 16777216 | tf_op jit(solution)/shard_map/mul | solution.py:158
  (97 shorter events, 8.4 us)
Async XLA Ops:
  33.7 8.5 %copy-start.4 = (bf16[1,64,64]{2,1,0:T(8,128)(2,1)S(1)}, bf16[1,64,64]{2,1,0:T(8,128)(2,1)}, u32[]{:S(2)}) copy-start(bf16[1,64,64]{2,1,0:T(8,128)(2,1)} %param.8) | copy-start | bytes 24580
  33.7 14.3 %copy-start.5 = (s32[1,4]{1,0:T(1,128)S(1)}, s32[1,4]{1,0:T(1,128)}, u32[]{:S(2)}) copy-start(s32[1,4]{1,0:T(1,128)} %param.9) | copy-start | bytes 52
  33.7 113.0 %all-to-all-start = ((bf16[16,2,16384]{2,1,0:T(2,128)(2,1)}), bf16[16,2,16384]{2,1,0:T(2,128)(2,1)S(1)}, u32[]{:S(2)}, u32[]{:S(2)}) async-start(bf16[16,2,16384]{2,1,0:T(2,128)(2,1)} %reshape.574), calls=%async_computation | async-start | bytes 2097152 | tf_op jit(solution)/shard_map/all_to_all | solution.py:95
  42.2 51.4 %collective-permute-start.1 = (bf16[1,64,64]{2,1,0:T(8,128)(2,1)S(1)}, bf16[1,64,64]{2,1,0:T(8,128)(2,1)S(1)}, u32[]{:S(2)}, u32[]{:S(2)}) collective-permute-start(bf16[1,64,64]{2,1,0:T(8,128)(2,1)S(1)} %copy-done.4), channel_id=1, source_target_pairs={{0,30},{2,0},{4,2},{6,4},{8,6},{10,8},{12,10},{14,12},{16,14},{18,... | collective-permute-start | bytes 24584 | tf_op jit(solution)/shard_map/ppermute | solution.py:122
  47.8 47.6 %collective-permute-start = (bf16[1,64,64]{2,1,0:T(8,128)(2,1)S(1)}, bf16[1,64,64]{2,1,0:T(8,128)(2,1)S(1)}, u32[]{:S(2)}, u32[]{:S(2)}) collective-permute-start(bf16[1,64,64]{2,1,0:T(8,128)(2,1)S(1)} %copy-done.4), channel_id=1, source_target_pairs={{0,2},{2,4},{4,6},{6,8},{8,10},{10,12},{12,14},{14,16},{16,18},{18... | collective-permute-start | bytes 24584 | tf_op jit(solution)/shard_map/ppermute | solution.py:115
  93.6 3.7 %collective-permute-start.3 = (bf16[1,64,64]{2,1,0:T(8,128)(2,1)S(1)}, bf16[1,64,64]{2,1,0:T(8,128)(2,1)S(1)}, u32[]{:S(2)}, u32[]{:S(2)}) collective-permute-start(bf16[1,64,64]{2,1,0:T(8,128)(2,1)S(1)} %collective-permute-done.1), channel_id=1, source_target_pairs={{0,30},{2,0},{4,2},{6,4},{8,6},{10,8},{12,10},{14,12},{16,14},{18,... | collective-permute-start | bytes 24584 | tf_op jit(solution)/shard_map/ppermute | solution.py:122
  95.4 7.3 %collective-permute-start.2 = (bf16[1,64,64]{2,1,0:T(8,128)(2,1)S(1)}, bf16[1,64,64]{2,1,0:T(8,128)(2,1)S(1)}, u32[]{:S(2)}, u32[]{:S(2)}) collective-permute-start(bf16[1,64,64]{2,1,0:T(8,128)(2,1)S(1)} %collective-permute-done), channel_id=1, source_target_pairs={{0,2},{2,4},{4,6},{6,8},{8,10},{10,12},{12,14},{14,16},{16,18},{18... | collective-permute-start | bytes 24584 | tf_op jit(solution)/shard_map/ppermute | solution.py:115
  97.4 6.8 %collective-permute-start.5 = (bf16[1,64,64]{2,1,0:T(8,128)(2,1)S(1)}, bf16[1,64,64]{2,1,0:T(8,128)(2,1)S(1)}, u32[]{:S(2)}, u32[]{:S(2)}) collective-permute-start(bf16[1,64,64]{2,1,0:T(8,128)(2,1)S(1)} %collective-permute-done.3), channel_id=1, source_target_pairs={{0,30},{2,0},{4,2},{6,4},{8,6},{10,8},{12,10},{14,12},{16,14},{18,... | collective-permute-start | bytes 24584 | tf_op jit(solution)/shard_map/ppermute | solution.py:122
  102.7 7.3 %collective-permute-start.4 = (bf16[1,64,64]{2,1,0:T(8,128)(2,1)S(1)}, bf16[1,64,64]{2,1,0:T(8,128)(2,1)S(1)}, u32[]{:S(2)}, u32[]{:S(2)}) collective-permute-start(bf16[1,64,64]{2,1,0:T(8,128)(2,1)S(1)} %collective-permute-done.2), channel_id=1, source_target_pairs={{0,2},{2,4},{4,6},{6,8},{8,10},{10,12},{12,14},{14,16},{16,18},{18... | collective-permute-start | bytes 24584 | tf_op jit(solution)/shard_map/ppermute | solution.py:115
  104.1 7.3 %collective-permute-start.7 = (bf16[1,64,64]{2,1,0:T(8,128)(2,1)S(1)}, bf16[1,64,64]{2,1,0:T(8,128)(2,1)S(1)}, u32[]{:S(2)}, u32[]{:S(2)}) collective-permute-start(bf16[1,64,64]{2,1,0:T(8,128)(2,1)S(1)} %collective-permute-done.5), channel_id=1, source_target_pairs={{0,30},{2,0},{4,2},{6,4},{8,6},{10,8},{12,10},{14,12},{16,14},{18,... | collective-permute-start | bytes 24584 | tf_op jit(solution)/shard_map/ppermute | solution.py:122
  110.0 7.3 %collective-permute-start.6 = (bf16[1,64,64]{2,1,0:T(8,128)(2,1)S(1)}, bf16[1,64,64]{2,1,0:T(8,128)(2,1)S(1)}, u32[]{:S(2)}, u32[]{:S(2)}) collective-permute-start(bf16[1,64,64]{2,1,0:T(8,128)(2,1)S(1)} %collective-permute-done.4), channel_id=1, source_target_pairs={{0,2},{2,4},{4,6},{6,8},{8,10},{10,12},{12,14},{14,16},{16,18},{18... | collective-permute-start | bytes 24584 | tf_op jit(solution)/shard_map/ppermute | solution.py:115
  111.5 7.3 %collective-permute-start.9 = (bf16[1,64,64]{2,1,0:T(8,128)(2,1)S(1)}, bf16[1,64,64]{2,1,0:T(8,128)(2,1)S(1)}, u32[]{:S(2)}, u32[]{:S(2)}) collective-permute-start(bf16[1,64,64]{2,1,0:T(8,128)(2,1)S(1)} %collective-permute-done.7), channel_id=1, source_target_pairs={{0,30},{2,0},{4,2},{6,4},{8,6},{10,8},{12,10},{14,12},{16,14},{18,... | collective-permute-start | bytes 24584 | tf_op jit(solution)/shard_map/ppermute | solution.py:122
  117.4 7.3 %collective-permute-start.8 = (bf16[1,64,64]{2,1,0:T(8,128)(2,1)S(1)}, bf16[1,64,64]{2,1,0:T(8,128)(2,1)S(1)}, u32[]{:S(2)}, u32[]{:S(2)}) collective-permute-start(bf16[1,64,64]{2,1,0:T(8,128)(2,1)S(1)} %collective-permute-done.6), channel_id=1, source_target_pairs={{0,2},{2,4},{4,6},{6,8},{8,10},{10,12},{12,14},{14,16},{16,18},{18... | collective-permute-start | bytes 24584 | tf_op jit(solution)/shard_map/ppermute | solution.py:115
  118.8 7.3 %collective-permute-start.11 = (bf16[1,64,64]{2,1,0:T(8,128)(2,1)S(1)}, bf16[1,64,64]{2,1,0:T(8,128)(2,1)S(1)}, u32[]{:S(2)}, u32[]{:S(2)}) collective-permute-start(bf16[1,64,64]{2,1,0:T(8,128)(2,1)S(1)} %collective-permute-done.9), channel_id=1, source_target_pairs={{0,30},{2,0},{4,2},{6,4},{8,6},{10,8},{12,10},{14,12},{16,14},{18,... | collective-permute-start | bytes 24584 | tf_op jit(solution)/shard_map/ppermute | solution.py:122
  124.7 7.3 %collective-permute-start.10 = (bf16[1,64,64]{2,1,0:T(8,128)(2,1)S(1)}, bf16[1,64,64]{2,1,0:T(8,128)(2,1)S(1)}, u32[]{:S(2)}, u32[]{:S(2)}) collective-permute-start(bf16[1,64,64]{2,1,0:T(8,128)(2,1)S(1)} %collective-permute-done.8), channel_id=1, source_target_pairs={{0,2},{2,4},{4,6},{6,8},{8,10},{10,12},{12,14},{14,16},{16,18},{18... | collective-permute-start | bytes 24584 | tf_op jit(solution)/shard_map/ppermute | solution.py:115
  126.1 13.2 %collective-permute-start.13 = (bf16[1,64,64]{2,1,0:T(8,128)(2,1)S(1)}, bf16[1,64,64]{2,1,0:T(8,128)(2,1)S(1)}, u32[]{:S(2)}, u32[]{:S(2)}) collective-permute-start(bf16[1,64,64]{2,1,0:T(8,128)(2,1)S(1)} %collective-permute-done.11), channel_id=1, source_target_pairs={{0,30},{2,0},{4,2},{6,4},{8,6},{10,8},{12,10},{14,12},{16,14},{18,... | collective-permute-start | bytes 24584 | tf_op jit(solution)/shard_map/ppermute | solution.py:122
  132.0 7.3 %collective-permute-start.12 = (bf16[1,64,64]{2,1,0:T(8,128)(2,1)S(1)}, bf16[1,64,64]{2,1,0:T(8,128)(2,1)S(1)}, u32[]{:S(2)}, u32[]{:S(2)}) collective-permute-start(bf16[1,64,64]{2,1,0:T(8,128)(2,1)S(1)} %collective-permute-done.10), channel_id=1, source_target_pairs={{0,2},{2,4},{4,6},{6,8},{8,10},{10,12},{12,14},{14,16},{16,18},{18... | collective-permute-start | bytes 24584 | tf_op jit(solution)/shard_map/ppermute | solution.py:115
  139.4 7.3 %collective-permute-start.14 = (bf16[1,64,64]{2,1,0:T(8,128)(2,1)S(1)}, bf16[1,64,64]{2,1,0:T(8,128)(2,1)S(1)}, u32[]{:S(2)}, u32[]{:S(2)}) collective-permute-start(bf16[1,64,64]{2,1,0:T(8,128)(2,1)S(1)} %collective-permute-done.12), channel_id=1, source_target_pairs={{0,2},{2,4},{4,6},{6,8},{8,10},{10,12},{12,14},{14,16},{16,18},{18... | collective-permute-start | bytes 24584 | tf_op jit(solution)/shard_map/ppermute | solution.py:115
  184.5 1.0 copy-start
  194.5 1.7 copy-start.1
  196.2 1.0 copy-start
  206.2 1.7 copy-start.1
  207.9 1.2 copy-start.2
  213.6 19.2 %all-to-all-start.1 = ((bf16[2,1,256,1024]{3,0,1,2:T(2,128)(2,1)}), bf16[2,1,256,1024]{3,0,1,2:T(2,128)(2,1)S(1)}, u32[]{:S(2)}, u32[]{:S(2)}) async-start(bf16[2,1,256,1024]{3,0,1,2:T(2,128)(2,1)} %copy.155), calls=%async_computation.1 | async-start | bytes 2097152 | tf_op jit(solution)/shard_map/all_to_all | solution.py:148
  217.2 69.6 %all-gather.3.cloned.1.call-start = ((), (), s32[]{:S(2)}) async-start(), calls=%async_computation.3 | async-start | bytes 3145728 | tf_op jit(solution)/shard_map/all_gather | solution.py:156
  234.5 1.1 copy-start.3
Sparse Core Ops, SparseCore 0:
  277.9 8.8 all-gather.2
